TPU v7x, 32 devices: a whole 2x2x4 slice. The times are simulated.
32 devices in a mesh: section: 4 (over y, x), row: 2 (over core), col: 4 (over z).
Axes of the slice: x: 2, y: 2, z: 4, core: 2. Of those that a mesh axis runs over, the one named last changes fastest.
Arguments:
- cotangent: float32 [4, 128, 4096], P('section', None, ('row', 'col')), may hold values from -6 to 6
- incoming: float32 [4, 128, 4096], P('section', None, ('row', 'col')), may hold values from -6 to 6
- upd_u: float32 [4, 8, 128, 4096], P('section', None, None, ('row', 'col')), may hold values from -4 to 4
- upd_v: float32 [4, 8, 128, 4096], P('section', None, None, ('row', 'col')), may hold values from -0.0078125 to 0.0078125
- saved_x: bfloat16 [4, 4, 128, 4096], P('section', None, None, ('row', 'col')), may hold values from -6 to 6
- saved_h: bfloat16 [4, 4, 2, 128, 14336], P('section', None, None, None, 'col'), may hold values from -6 to 6
- norm_gain: float32 [4, 4096], P('section', ('row', 'col')), may hold values from 0.25 to 1.75
- w_gate: bfloat16 [4, 4096, 14336], P('section', 'row', 'col'), may hold values from -0.09375 to 0.09375
- w_up: bfloat16 [4, 4096, 14336], P('section', 'row', 'col'), may hold values from -0.09375 to 0.09375
- w_down: bfloat16 [4, 14336, 4096], P('section', 'col', 'row'), may hold values from -0.046875 to 0.046875
Outputs:
- new_cotangent: float32 [4, 128, 4096], P('section', None, ('row', 'col'))
- residual_out: float32 [4, 128, 4096], P('section', None, ('row', 'col'))
All inputs are finite; a program needn't handle non-finite values.
Results may differ from a plain program's by a relative error of at most 0.014.
Values may be sent and summed in bfloat16 or wider, within the bound.
No kernel may reach another device: no remote copies, remote signals or barrier semaphores. Data moves between devices by JAX's collectives and lax.ppermute only.
A program may use at most 128 MiB of HBM per device.

v0:
```python
import jax
import jax.numpy as jnp
from jax import lax
from jax.sharding import PartitionSpec as P

D = 4096
eps = 1e-05


def shifted(x, axis, by):
    devices = lax.axis_size(axis)
    return lax.ppermute(x, axis, [(i, (i + by) % devices) for i in range(devices)])


def rotate(carry):
    return shifted(carry, "section", -1)


def shards(cotangent, incoming, upd_u, upd_v, saved_x, saved_h, norm_gain, w_gate, w_up, w_down):
    sections = lax.axis_size("section")
    section_idx = lax.axis_index("section")
    inputs_all = saved_x[0].astype(jnp.float32)
    hidden_all = saved_h[0]
    gain = norm_gain[0]
    wg = w_gate[0]
    wu = w_up[0]
    wd = w_down[0]

    def layer_step(step, carry):
        carry = rotate(carry)
        micro = (section_idx + step + 1) % sections
        xf = lax.dynamic_index_in_dim(inputs_all, micro, 0, keepdims=False)
        hpair = lax.dynamic_index_in_dim(hidden_all, micro, 0, keepdims=False)
        sumsq = lax.psum(jnp.sum(xf * xf, axis=1), ("row", "col"))
        gy = carry.astype(jnp.bfloat16)
        wide = lax.all_gather(gy, "col", axis=1, tiled=True)
        ga_part = lax.dot_general(
            wide, wd, (((1,), (1,)), ((), ())), preferred_element_type=jnp.float32
        )
        ga = lax.psum_scatter(ga_part, "row", scatter_dimension=1, tiled=True)
        width = ga.shape[1]
        offset = lax.axis_index("row") * width
        hg = lax.dynamic_slice_in_dim(hpair[0], offset, width, 1).astype(jnp.float32)
        hu = lax.dynamic_slice_in_dim(hpair[1], offset, width, 1).astype(jnp.float32)
        sig = jax.nn.sigmoid(hg)
        part_gate = (ga * hu * sig * (1.0 + hg * (1.0 - sig))).astype(jnp.bfloat16)
        part_up = (ga * hg * sig).astype(jnp.bfloat16)
        grad_gate, grad_up = (
            lax.all_gather(part_gate, "row", axis=1, tiled=True),
            lax.all_gather(part_up, "row", axis=1, tiled=True),
        )
        first = lax.dot_general(
            wg, grad_gate, (((1,), (1,)), ((), ())), preferred_element_type=jnp.float32
        )
        second = lax.dot_general(
            wu, grad_up, (((1,), (1,)), ((), ())), preferred_element_type=jnp.float32
        )
        normgrad = lax.psum_scatter(first + second, "col", scatter_dimension=0, tiled=True).T
        rstd = lax.rsqrt(sumsq / D + eps)[:, None]
        scaled = gain * normgrad
        inner = lax.psum(jnp.sum(scaled * xf, axis=1), ("row", "col"))[:, None] / D
        updated = carry + rstd * scaled - xf * (rstd * rstd * rstd) * inner
        active = jnp.logical_and(step >= micro, step - micro < sections)
        return jnp.where(active, updated, carry)

    pulled = lax.fori_loop(0, 2 * sections - 1, layer_step, cotangent[0])
    pulled = rotate(pulled)
    resid = pulled + incoming[0] - cotangent[0]
    local_dots = jnp.einsum("urd,rd->u", upd_v[0], resid, precision=lax.Precision.HIGHEST)
    dots = lax.psum(local_dots, ("row", "col"))
    update = jnp.einsum("u,urd->rd", dots, upd_u[0], precision=lax.Precision.HIGHEST)
    fresh = cotangent[0] + resid - update
    return (fresh[None], resid[None])


def solution(mesh):
    placed = (
        P("section", None, ("row", "col")),
        P("section", None, ("row", "col")),
        P("section", None, None, ("row", "col")),
        P("section", None, None, ("row", "col")),
        P("section", None, None, ("row", "col")),
        P("section", None, None, None, "col"),
        P("section", ("row", "col")),
        P("section", "row", "col"),
        P("section", "row", "col"),
        P("section", "col", "row"),
    )
    return jax.shard_map(
        shards,
        mesh=mesh,
        in_specs=placed,
        out_specs=(P("section", None, ("row", "col")), P("section", None, ("row", "col"))),
        check_vma=False,
    )
```

profile of v0, /device:TPU:0, one launch (start us, length us, event | category | flops | bytes accessed | tf_op | source)
XLA Modules:
  0.0 880.5 jit_solution(12553855589407518897)
XLA Ops:
  10.2 832.8 %while.15 = (s32[]{:T(128)}, f32[128,512]{1,0:T(8,128)}, s32[]{:T(128)}, f32[4,128,512]{2,1,0:T(8,128)S(1)}, f32[1,512]{1,0:T(1,128)}, /*index=5*/bf16[3584,2048...) while((s32[]{:T(128)}, f32[128,512]{1,0:T(8,128)}, ...), condition=%wide.region_7.8_spmd, body=%wide.region_0.7_spmd.sunk | while | flops 5641699840 | bytes 72765032 | solution.py:66
  10.2 4.0 collective-permute-start
  14.2 5.9 collective-permute-done
  20.1 15.1 %all_gather.33 = bf16[128,2048]{1,0:T(8,128)(2,1)S(1)} all-gather(bf16[128,512]{1,0:T(8,128)(2,1)S(1)} %convert_element_type.72), channel_id=1, replica_groups=mesh['section'=4,'row'=2,'col'=4] {'col'}, dimensions={1}, use_global_device_ids=true | all-gather | bytes 655360 | tf_op jit(solution)/shard_map/while/body/eval_jaxpr/all_gather | solution.py:36
  35.3 11.4 %fusion.48 = f32[128,3584]{1,0:T(8,128)} fusion(bf16[128,2048]{1,0:T(8,128)(2,1)S(1)} %all_gather.33, bf16[3584,2048]{1,0:T(8,128)(2,1)} %get-tuple-element.365), kind=kOutput, calls=%fused_computation.40.clone.1 | convolution fusion | flops 1879048192 | bytes 17039360 | tf_op jit(solution)/shard_map/while/body/eval_jaxpr/dot_general | solution.py:37
  46.7 12.0 %reduce-scatter.3.cloned.1.call-done = f32[128,1792]{1,0:T(8,128)} async-done(((f32[128,3584]{1,0:T(8,128)}), f32[128,1792]{1,0:T(8,128)}) %reduce-scatter.3.cloned.1.call-update) | async-done | bytes 917520 | tf_op jit(solution)/shard_map/while/body/eval_jaxpr/reduce_scatter | solution.py:40
  60.6 2.5 all_gather.34
  65.5 9.9 %fusion.50 = f32[128,2048]{1,0:T(8,128)S(1)} fusion(bf16[128,3584]{1,0:T(8,128)(2,1)S(1)} %all_gather.34, bf16[2048,3584]{1,0:T(8,128)(2,1)} %get-tuple-element.367), kind=kOutput, calls=%fused_computation.41.clone.1 | convolution fusion | flops 1879048192 | bytes 16646144 | tf_op jit(solution)/shard_map/while/body/eval_jaxpr/dot_general | solution.py:52
  75.4 10.9 %fusion.51 = f32[2048,128]{0,1:T(8,128)} fusion(f32[128,2048]{1,0:T(8,128)S(1)} %fusion.50, bf16[128,3584]{1,0:T(8,128)(2,1)S(1)} %all_gather.35, bf16[2048,3584]{1,0:T(8,128)(2,1)} %get-tuple-element.368), kind=kOutput, calls=%fused_computation.1.clone.1 | convolution fusion | flops 1879310336 | bytes 17694720 | tf_op jit(solution)/shard_map/while/body/eval_jaxpr/dot_general | solution.py:55
  86.4 28.7 %reduce-scatter.5.cloned.1.call-done = f32[512,128]{0,1:T(8,128)} async-done(((f32[2048,128]{0,1:T(8,128)}), f32[512,128]{0,1:T(8,128)}) %reduce-scatter.5.cloned.1.call-update) | async-done | bytes 262160 | tf_op jit(solution)/shard_map/while/body/eval_jaxpr/reduce_scatter | solution.py:58
  116.2 13.7 %all-reduce.2 = (f32[128]{0:T(128)S(1)}, f32[128]{0:T(128)S(1)}) all-reduce(f32[128]{0:T(128)S(1)} %get-tuple-element.317, f32[128]{0:T(128)S(1)} %get-tuple-element.318), channel_id=1, replica_groups=mesh['section'=4,'row'=2,'col'=4] {'row','col'}, use_global_device_ids=true, to_apply=%region_6.6 | all-reduce | flops 256 | bytes 2048 | tf_op jit(solution)/shard_map/while/body/eval_jaxpr/psum | solution.py:61
  134.1 7.0 collective-permute-done
  141.1 16.1 %all_gather.33 = bf16[128,2048]{1,0:T(8,128)(2,1)S(1)} all-gather(bf16[128,512]{1,0:T(8,128)(2,1)S(1)} %convert_element_type.72), channel_id=1, replica_groups=mesh['section'=4,'row'=2,'col'=4] {'col'}, dimensions={1}, use_global_device_ids=true | all-gather | bytes 655360 | tf_op jit(solution)/shard_map/while/body/eval_jaxpr/all_gather | solution.py:36
  157.2 11.3 %fusion.48 = f32[128,3584]{1,0:T(8,128)} fusion(bf16[128,2048]{1,0:T(8,128)(2,1)S(1)} %all_gather.33, bf16[3584,2048]{1,0:T(8,128)(2,1)} %get-tuple-element.365), kind=kOutput, calls=%fused_computation.40.clone.1 | convolution fusion | flops 1879048192 | bytes 17039360 | tf_op jit(solution)/shard_map/while/body/eval_jaxpr/dot_general | solution.py:37
  168.7 8.6 reduce-scatter.3.cloned.1.call-done
  184.1 9.9 %fusion.50 = f32[128,2048]{1,0:T(8,128)S(1)} fusion(bf16[128,3584]{1,0:T(8,128)(2,1)S(1)} %all_gather.34, bf16[2048,3584]{1,0:T(8,128)(2,1)} %get-tuple-element.367), kind=kOutput, calls=%fused_computation.41.clone.1 | convolution fusion | flops 1879048192 | bytes 16646144 | tf_op jit(solution)/shard_map/while/body/eval_jaxpr/dot_general | solution.py:52
  194.0 10.9 %fusion.51 = f32[2048,128]{0,1:T(8,128)} fusion(f32[128,2048]{1,0:T(8,128)S(1)} %fusion.50, bf16[128,3584]{1,0:T(8,128)(2,1)S(1)} %all_gather.35, bf16[2048,3584]{1,0:T(8,128)(2,1)} %get-tuple-element.368), kind=kOutput, calls=%fused_computation.1.clone.1 | convolution fusion | flops 1879310336 | bytes 17694720 | tf_op jit(solution)/shard_map/while/body/eval_jaxpr/dot_general | solution.py:55
  205.0 28.7 %reduce-scatter.5.cloned.1.call-done = f32[512,128]{0,1:T(8,128)} async-done(((f32[2048,128]{0,1:T(8,128)}), f32[512,128]{0,1:T(8,128)}) %reduce-scatter.5.cloned.1.call-update) | async-done | bytes 262160 | tf_op jit(solution)/shard_map/while/body/eval_jaxpr/reduce_scatter | solution.py:58
  234.8 13.7 %all-reduce.2 = (f32[128]{0:T(128)S(1)}, f32[128]{0:T(128)S(1)}) all-reduce(f32[128]{0:T(128)S(1)} %get-tuple-element.317, f32[128]{0:T(128)S(1)} %get-tuple-element.318), channel_id=1, replica_groups=mesh['section'=4,'row'=2,'col'=4] {'row','col'}, use_global_device_ids=true, to_apply=%region_6.6 | all-reduce | flops 256 | bytes 2048 | tf_op jit(solution)/shard_map/while/body/eval_jaxpr/psum | solution.py:61
  252.7 7.0 collective-permute-done
  259.7 16.2 %all_gather.33 = bf16[128,2048]{1,0:T(8,128)(2,1)S(1)} all-gather(bf16[128,512]{1,0:T(8,128)(2,1)S(1)} %convert_element_type.72), channel_id=1, replica_groups=mesh['section'=4,'row'=2,'col'=4] {'col'}, dimensions={1}, use_global_device_ids=true | all-gather | bytes 655360 | tf_op jit(solution)/shard_map/while/body/eval_jaxpr/all_gather | solution.py:36
  275.8 11.3 %fusion.48 = f32[128,3584]{1,0:T(8,128)} fusion(bf16[128,2048]{1,0:T(8,128)(2,1)S(1)} %all_gather.33, bf16[3584,2048]{1,0:T(8,128)(2,1)} %get-tuple-element.365), kind=kOutput, calls=%fused_computation.40.clone.1 | convolution fusion | flops 1879048192 | bytes 17039360 | tf_op jit(solution)/shard_map/while/body/eval_jaxpr/dot_general | solution.py:37
  287.3 8.5 reduce-scatter.3.cloned.1.call-done
  302.6 9.9 %fusion.50 = f32[128,2048]{1,0:T(8,128)S(1)} fusion(bf16[128,3584]{1,0:T(8,128)(2,1)S(1)} %all_gather.34, bf16[2048,3584]{1,0:T(8,128)(2,1)} %get-tuple-element.367), kind=kOutput, calls=%fused_computation.41.clone.1 | convolution fusion | flops 1879048192 | bytes 16646144 | tf_op jit(solution)/shard_map/while/body/eval_jaxpr/dot_general | solution.py:52
  312.6 10.9 %fusion.51 = f32[2048,128]{0,1:T(8,128)} fusion(f32[128,2048]{1,0:T(8,128)S(1)} %fusion.50, bf16[128,3584]{1,0:T(8,128)(2,1)S(1)} %all_gather.35, bf16[2048,3584]{1,0:T(8,128)(2,1)} %get-tuple-element.368), kind=kOutput, calls=%fused_computation.1.clone.1 | convolution fusion | flops 1879310336 | bytes 17694720 | tf_op jit(solution)/shard_map/while/body/eval_jaxpr/dot_general | solution.py:55
  323.5 28.7 %reduce-scatter.5.cloned.1.call-done = f32[512,128]{0,1:T(8,128)} async-done(((f32[2048,128]{0,1:T(8,128)}), f32[512,128]{0,1:T(8,128)}) %reduce-scatter.5.cloned.1.call-update) | async-done | bytes 262160 | tf_op jit(solution)/shard_map/while/body/eval_jaxpr/reduce_scatter | solution.py:58
  353.3 13.7 %all-reduce.2 = (f32[128]{0:T(128)S(1)}, f32[128]{0:T(128)S(1)}) all-reduce(f32[128]{0:T(128)S(1)} %get-tuple-element.317, f32[128]{0:T(128)S(1)} %get-tuple-element.318), channel_id=1, replica_groups=mesh['section'=4,'row'=2,'col'=4] {'row','col'}, use_global_device_ids=true, to_apply=%region_6.6 | all-reduce | flops 256 | bytes 2048 | tf_op jit(solution)/shard_map/while/body/eval_jaxpr/psum | solution.py:61
  371.2 7.0 collective-permute-done
  378.2 16.2 %all_gather.33 = bf16[128,2048]{1,0:T(8,128)(2,1)S(1)} all-gather(bf16[128,512]{1,0:T(8,128)(2,1)S(1)} %convert_element_type.72), channel_id=1, replica_groups=mesh['section'=4,'row'=2,'col'=4] {'col'}, dimensions={1}, use_global_device_ids=true | all-gather | bytes 655360 | tf_op jit(solution)/shard_map/while/body/eval_jaxpr/all_gather | solution.py:36
  394.4 11.3 %fusion.48 = f32[128,3584]{1,0:T(8,128)} fusion(bf16[128,2048]{1,0:T(8,128)(2,1)S(1)} %all_gather.33, bf16[3584,2048]{1,0:T(8,128)(2,1)} %get-tuple-element.365), kind=kOutput, calls=%fused_computation.40.clone.1 | convolution fusion | flops 1879048192 | bytes 17039360 | tf_op jit(solution)/shard_map/while/body/eval_jaxpr/dot_general | solution.py:37
  405.8 8.5 reduce-scatter.3.cloned.1.call-done
  416.2 2.5 all_gather.34
  421.2 9.9 %fusion.50 = f32[128,2048]{1,0:T(8,128)S(1)} fusion(bf16[128,3584]{1,0:T(8,128)(2,1)S(1)} %all_gather.34, bf16[2048,3584]{1,0:T(8,128)(2,1)} %get-tuple-element.367), kind=kOutput, calls=%fused_computation.41.clone.1 | convolution fusion | flops 1879048192 | bytes 16646144 | tf_op jit(solution)/shard_map/while/body/eval_jaxpr/dot_general | solution.py:52
  431.1 10.9 %fusion.51 = f32[2048,128]{0,1:T(8,128)} fusion(f32[128,2048]{1,0:T(8,128)S(1)} %fusion.50, bf16[128,3584]{1,0:T(8,128)(2,1)S(1)} %all_gather.35, bf16[2048,3584]{1,0:T(8,128)(2,1)} %get-tuple-element.368), kind=kOutput, calls=%fused_computation.1.clone.1 | convolution fusion | flops 1879310336 | bytes 17694720 | tf_op jit(solution)/shard_map/while/body/eval_jaxpr/dot_general | solution.py:55
  442.0 28.7 %reduce-scatter.5.cloned.1.call-done = f32[512,128]{0,1:T(8,128)} async-done(((f32[2048,128]{0,1:T(8,128)}), f32[512,128]{0,1:T(8,128)}) %reduce-scatter.5.cloned.1.call-update) | async-done | bytes 262160 | tf_op jit(solution)/shard_map/while/body/eval_jaxpr/reduce_scatter | solution.py:58
  471.8 13.7 %all-reduce.2 = (f32[128]{0:T(128)S(1)}, f32[128]{0:T(128)S(1)}) all-reduce(f32[128]{0:T(128)S(1)} %get-tuple-element.317, f32[128]{0:T(128)S(1)} %get-tuple-element.318), channel_id=1, replica_groups=mesh['section'=4,'row'=2,'col'=4] {'row','col'}, use_global_device_ids=true, to_apply=%region_6.6 | all-reduce | flops 256 | bytes 2048 | tf_op jit(solution)/shard_map/while/body/eval_jaxpr/psum | solution.py:61
  489.7 7.0 collective-permute-done
  496.7 16.2 %all_gather.33 = bf16[128,2048]{1,0:T(8,128)(2,1)S(1)} all-gather(bf16[128,512]{1,0:T(8,128)(2,1)S(1)} %convert_element_type.72), channel_id=1, replica_groups=mesh['section'=4,'row'=2,'col'=4] {'col'}, dimensions={1}, use_global_device_ids=true | all-gather | bytes 655360 | tf_op jit(solution)/shard_map/while/body/eval_jaxpr/all_gather | solution.py:36
  512.9 11.3 %fusion.48 = f32[128,3584]{1,0:T(8,128)} fusion(bf16[128,2048]{1,0:T(8,128)(2,1)S(1)} %all_gather.33, bf16[3584,2048]{1,0:T(8,128)(2,1)} %get-tuple-element.365), kind=kOutput, calls=%fused_computation.40.clone.1 | convolution fusion | flops 1879048192 | bytes 17039360 | tf_op jit(solution)/shard_map/while/body/eval_jaxpr/dot_general | solution.py:37
  524.4 8.5 reduce-scatter.3.cloned.1.call-done
  534.8 2.5 all_gather.34
  539.7 9.9 %fusion.50 = f32[128,2048]{1,0:T(8,128)S(1)} fusion(bf16[128,3584]{1,0:T(8,128)(2,1)S(1)} %all_gather.34, bf16[2048,3584]{1,0:T(8,128)(2,1)} %get-tuple-element.367), kind=kOutput, calls=%fused_computation.41.clone.1 | convolution fusion | flops 1879048192 | bytes 16646144 | tf_op jit(solution)/shard_map/while/body/eval_jaxpr/dot_general | solution.py:52
  549.6 10.9 %fusion.51 = f32[2048,128]{0,1:T(8,128)} fusion(f32[128,2048]{1,0:T(8,128)S(1)} %fusion.50, bf16[128,3584]{1,0:T(8,128)(2,1)S(1)} %all_gather.35, bf16[2048,3584]{1,0:T(8,128)(2,1)} %get-tuple-element.368), kind=kOutput, calls=%fused_computation.1.clone.1 | convolution fusion | flops 1879310336 | bytes 17694720 | tf_op jit(solution)/shard_map/while/body/eval_jaxpr/dot_general | solution.py:55
  560.6 28.7 %reduce-scatter.5.cloned.1.call-done = f32[512,128]{0,1:T(8,128)} async-done(((f32[2048,128]{0,1:T(8,128)}), f32[512,128]{0,1:T(8,128)}) %reduce-scatter.5.cloned.1.call-update) | async-done | bytes 262160 | tf_op jit(solution)/shard_map/while/body/eval_jaxpr/reduce_scatter | solution.py:58
  590.4 13.7 %all-reduce.2 = (f32[128]{0:T(128)S(1)}, f32[128]{0:T(128)S(1)}) all-reduce(f32[128]{0:T(128)S(1)} %get-tuple-element.317, f32[128]{0:T(128)S(1)} %get-tuple-element.318), channel_id=1, replica_groups=mesh['section'=4,'row'=2,'col'=4] {'row','col'}, use_global_device_ids=true, to_apply=%region_6.6 | all-reduce | flops 256 | bytes 2048 | tf_op jit(solution)/shard_map/while/body/eval_jaxpr/psum | solution.py:61
  608.3 7.0 collective-permute-done
  615.3 16.2 %all_gather.33 = bf16[128,2048]{1,0:T(8,128)(2,1)S(1)} all-gather(bf16[128,512]{1,0:T(8,128)(2,1)S(1)} %convert_element_type.72), channel_id=1, replica_groups=mesh['section'=4,'row'=2,'col'=4] {'col'}, dimensions={1}, use_global_device_ids=true | all-gather | bytes 655360 | tf_op jit(solution)/shard_map/while/body/eval_jaxpr/all_gather | solution.py:36
  631.5 11.3 %fusion.48 = f32[128,3584]{1,0:T(8,128)} fusion(bf16[128,2048]{1,0:T(8,128)(2,1)S(1)} %all_gather.33, bf16[3584,2048]{1,0:T(8,128)(2,1)} %get-tuple-element.365), kind=kOutput, calls=%fused_computation.40.clone.1 | convolution fusion | flops 1879048192 | bytes 17039360 | tf_op jit(solution)/shard_map/while/body/eval_jaxpr/dot_general | solution.py:37
  642.9 8.5 reduce-scatter.3.cloned.1.call-done
  658.2 9.9 %fusion.50 = f32[128,2048]{1,0:T(8,128)S(1)} fusion(bf16[128,3584]{1,0:T(8,128)(2,1)S(1)} %all_gather.34, bf16[2048,3584]{1,0:T(8,128)(2,1)} %get-tuple-element.367), kind=kOutput, calls=%fused_computation.41.clone.1 | convolution fusion | flops 1879048192 | bytes 16646144 | tf_op jit(solution)/shard_map/while/body/eval_jaxpr/dot_general | solution.py:52
  668.1 10.9 %fusion.51 = f32[2048,128]{0,1:T(8,128)} fusion(f32[128,2048]{1,0:T(8,128)S(1)} %fusion.50, bf16[128,3584]{1,0:T(8,128)(2,1)S(1)} %all_gather.35, bf16[2048,3584]{1,0:T(8,128)(2,1)} %get-tuple-element.368), kind=kOutput, calls=%fused_computation.1.clone.1 | convolution fusion | flops 1879310336 | bytes 17694720 | tf_op jit(solution)/shard_map/while/body/eval_jaxpr/dot_general | solution.py:55
  679.1 28.7 %reduce-scatter.5.cloned.1.call-done = f32[512,128]{0,1:T(8,128)} async-done(((f32[2048,128]{0,1:T(8,128)}), f32[512,128]{0,1:T(8,128)}) %reduce-scatter.5.cloned.1.call-update) | async-done | bytes 262160 | tf_op jit(solution)/shard_map/while/body/eval_jaxpr/reduce_scatter | solution.py:58
  708.9 13.7 %all-reduce.2 = (f32[128]{0:T(128)S(1)}, f32[128]{0:T(128)S(1)}) all-reduce(f32[128]{0:T(128)S(1)} %get-tuple-element.317, f32[128]{0:T(128)S(1)} %get-tuple-element.318), channel_id=1, replica_groups=mesh['section'=4,'row'=2,'col'=4] {'row','col'}, use_global_device_ids=true, to_apply=%region_6.6 | all-reduce | flops 256 | bytes 2048 | tf_op jit(solution)/shard_map/while/body/eval_jaxpr/psum | solution.py:61
  726.8 7.0 collective-permute-done
  733.8 16.2 %all_gather.33 = bf16[128,2048]{1,0:T(8,128)(2,1)S(1)} all-gather(bf16[128,512]{1,0:T(8,128)(2,1)S(1)} %convert_element_type.72), channel_id=1, replica_groups=mesh['section'=4,'row'=2,'col'=4] {'col'}, dimensions={1}, use_global_device_ids=true | all-gather | bytes 655360 | tf_op jit(solution)/shard_map/while/body/eval_jaxpr/all_gather | solution.py:36
  750.0 11.3 %fusion.48 = f32[128,3584]{1,0:T(8,128)} fusion(bf16[128,2048]{1,0:T(8,128)(2,1)S(1)} %all_gather.33, bf16[3584,2048]{1,0:T(8,128)(2,1)} %get-tuple-element.365), kind=kOutput, calls=%fused_computation.40.clone.1 | convolution fusion | flops 1879048192 | bytes 17039360 | tf_op jit(solution)/shard_map/while/body/eval_jaxpr/dot_general | solution.py:37
  761.4 8.5 reduce-scatter.3.cloned.1.call-done
  776.7 9.9 %fusion.50 = f32[128,2048]{1,0:T(8,128)S(1)} fusion(bf16[128,3584]{1,0:T(8,128)(2,1)S(1)} %all_gather.34, bf16[2048,3584]{1,0:T(8,128)(2,1)} %get-tuple-element.367), kind=kOutput, calls=%fused_computation.41.clone.1 | convolution fusion | flops 1879048192 | bytes 16646144 | tf_op jit(solution)/shard_map/while/body/eval_jaxpr/dot_general | solution.py:52
  786.7 10.9 %fusion.51 = f32[2048,128]{0,1:T(8,128)} fusion(f32[128,2048]{1,0:T(8,128)S(1)} %fusion.50, bf16[128,3584]{1,0:T(8,128)(2,1)S(1)} %all_gather.35, bf16[2048,3584]{1,0:T(8,128)(2,1)} %get-tuple-element.368), kind=kOutput, calls=%fused_computation.1.clone.1 | convolution fusion | flops 1879310336 | bytes 17694720 | tf_op jit(solution)/shard_map/while/body/eval_jaxpr/dot_general | solution.py:55
  797.6 28.7 %reduce-scatter.5.cloned.1.call-done = f32[512,128]{0,1:T(8,128)} async-done(((f32[2048,128]{0,1:T(8,128)}), f32[512,128]{0,1:T(8,128)}) %reduce-scatter.5.cloned.1.call-update) | async-done | bytes 262160 | tf_op jit(solution)/shard_map/while/body/eval_jaxpr/reduce_scatter | solution.py:58
  827.4 13.7 %all-reduce.2 = (f32[128]{0:T(128)S(1)}, f32[128]{0:T(128)S(1)}) all-reduce(f32[128]{0:T(128)S(1)} %get-tuple-element.317, f32[128]{0:T(128)S(1)} %get-tuple-element.318), channel_id=1, replica_groups=mesh['section'=4,'row'=2,'col'=4] {'row','col'}, use_global_device_ids=true, to_apply=%region_6.6 | all-reduce | flops 256 | bytes 2048 | tf_op jit(solution)/shard_map/while/body/eval_jaxpr/psum | solution.py:61
  845.3 7.0 collective-permute-done.1
  855.4 14.0 %psum.35 = f32[8]{0:T(128)S(1)} all-reduce(f32[8]{0:T(128)S(1)} %fusion.16), channel_id=1, replica_groups=mesh['section'=4,'row'=2,'col'=4] {'row','col'}, use_global_device_ids=true, to_apply=%region_8.9 | all-reduce | flops 8 | bytes 64 | tf_op jit(solution)/shard_map/psum | solution.py:70
  869.4 2.8 fusion.17
  (104 shorter events, 85.5 us)
Async XLA Ops:
  7.2 862.2 %copy-start = (f32[1,8,128,512]{3,2,1,0:T(8,128)S(1)}, f32[1,8,128,512]{3,2,1,0:T(8,128)}, u32[]{:S(2)}) copy-start(f32[1,8,128,512]{3,2,1,0:T(8,128)} %param.14) | copy-start | bytes 6291460
  10.2 48.5 %reduce-scatter.3.cloned.1.call-start = ((), (), s32[]{:S(2)}) async-start(), calls=%async_computation.2 | async-start | bytes 2752512 | tf_op jit(solution)/shard_map/while/body/eval_jaxpr/reduce_scatter | solution.py:40
  10.2 9.9 %collective-permute-start = (f32[128,512]{1,0:T(8,128)}, f32[128,512]{1,0:T(8,128)S(1)}, u32[]{:S(2)}, u32[]{:S(2)}) collective-permute-start(f32[128,512]{1,0:T(8,128)} %get-tuple-element.343), channel_id=1, source_target_pairs={{0,24},{8,0},{16,8},{24,16},{1,25},{9,1},{17,9},{25,17},{2,26},{10... | collective-permute-start | bytes 786440 | tf_op jit(solution)/shard_map/while/body/eval_jaxpr/ppermute | solution.py:12
  46.6 68.5 %reduce-scatter.5.cloned.1.call-start = ((), (), s32[]{:S(2)}) async-start(), calls=%async_computation.3 | async-start | bytes 1310720 | tf_op jit(solution)/shard_map/while/body/eval_jaxpr/reduce_scatter | solution.py:58
  75.4 39.7 %copy-start.2 = (f32[1,512]{1,0:T(1,128)S(1)}, f32[1,512]{1,0:T(1,128)}, u32[]{:S(2)}) copy-start(f32[1,512]{1,0:T(1,128)} %get-tuple-element.364) | copy-start | bytes 6148 | tf_op jit(solution)/shard_map/while
  131.7 45.6 %reduce-scatter.3.cloned.1.call-start = ((), (), s32[]{:S(2)}) async-start(), calls=%async_computation.2 | async-start | bytes 2752512 | tf_op jit(solution)/shard_map/while/body/eval_jaxpr/reduce_scatter | solution.py:40
  131.7 9.4 %collective-permute-start = (f32[128,512]{1,0:T(8,128)}, f32[128,512]{1,0:T(8,128)S(1)}, u32[]{:S(2)}, u32[]{:S(2)}) collective-permute-start(f32[128,512]{1,0:T(8,128)} %get-tuple-element.343), channel_id=1, source_target_pairs={{0,24},{8,0},{16,8},{24,16},{1,25},{9,1},{17,9},{25,17},{2,26},{10... | collective-permute-start | bytes 786440 | tf_op jit(solution)/shard_map/while/body/eval_jaxpr/ppermute | solution.py:12
  168.6 65.1 %reduce-scatter.5.cloned.1.call-start = ((), (), s32[]{:S(2)}) async-start(), calls=%async_computation.3 | async-start | bytes 1310720 | tf_op jit(solution)/shard_map/while/body/eval_jaxpr/reduce_scatter | solution.py:58
  194.0 39.7 %copy-start.2 = (f32[1,512]{1,0:T(1,128)S(1)}, f32[1,512]{1,0:T(1,128)}, u32[]{:S(2)}) copy-start(f32[1,512]{1,0:T(1,128)} %get-tuple-element.364) | copy-start | bytes 6148 | tf_op jit(solution)/shard_map/while
  250.3 45.6 %reduce-scatter.3.cloned.1.call-start = ((), (), s32[]{:S(2)}) async-start(), calls=%async_computation.2 | async-start | bytes 2752512 | tf_op jit(solution)/shard_map/while/body/eval_jaxpr/reduce_scatter | solution.py:40
  250.3 9.4 %collective-permute-start = (f32[128,512]{1,0:T(8,128)}, f32[128,512]{1,0:T(8,128)S(1)}, u32[]{:S(2)}, u32[]{:S(2)}) collective-permute-start(f32[128,512]{1,0:T(8,128)} %get-tuple-element.343), channel_id=1, source_target_pairs={{0,24},{8,0},{16,8},{24,16},{1,25},{9,1},{17,9},{25,17},{2,26},{10... | collective-permute-start | bytes 786440 | tf_op jit(solution)/shard_map/while/body/eval_jaxpr/ppermute | solution.py:12
  287.2 65.0 %reduce-scatter.5.cloned.1.call-start = ((), (), s32[]{:S(2)}) async-start(), calls=%async_computation.3 | async-start | bytes 1310720 | tf_op jit(solution)/shard_map/while/body/eval_jaxpr/reduce_scatter | solution.py:58
  312.6 39.7 %copy-start.2 = (f32[1,512]{1,0:T(1,128)S(1)}, f32[1,512]{1,0:T(1,128)}, u32[]{:S(2)}) copy-start(f32[1,512]{1,0:T(1,128)} %get-tuple-element.364) | copy-start | bytes 6148 | tf_op jit(solution)/shard_map/while
  368.8 45.5 %reduce-scatter.3.cloned.1.call-start = ((), (), s32[]{:S(2)}) async-start(), calls=%async_computation.2 | async-start | bytes 2752512 | tf_op jit(solution)/shard_map/while/body/eval_jaxpr/reduce_scatter | solution.py:40
  368.8 9.4 %collective-permute-start = (f32[128,512]{1,0:T(8,128)}, f32[128,512]{1,0:T(8,128)S(1)}, u32[]{:S(2)}, u32[]{:S(2)}) collective-permute-start(f32[128,512]{1,0:T(8,128)} %get-tuple-element.343), channel_id=1, source_target_pairs={{0,24},{8,0},{16,8},{24,16},{1,25},{9,1},{17,9},{25,17},{2,26},{10... | collective-permute-start | bytes 786440 | tf_op jit(solution)/shard_map/while/body/eval_jaxpr/ppermute | solution.py:12
  405.8 65.0 %reduce-scatter.5.cloned.1.call-start = ((), (), s32[]{:S(2)}) async-start(), calls=%async_computation.3 | async-start | bytes 1310720 | tf_op jit(solution)/shard_map/while/body/eval_jaxpr/reduce_scatter | solution.py:58
  431.1 39.7 %copy-start.2 = (f32[1,512]{1,0:T(1,128)S(1)}, f32[1,512]{1,0:T(1,128)}, u32[]{:S(2)}) copy-start(f32[1,512]{1,0:T(1,128)} %get-tuple-element.364) | copy-start | bytes 6148 | tf_op jit(solution)/shard_map/while
  487.4 45.5 %reduce-scatter.3.cloned.1.call-start = ((), (), s32[]{:S(2)}) async-start(), calls=%async_computation.2 | async-start | bytes 2752512 | tf_op jit(solution)/shard_map/while/body/eval_jaxpr/reduce_scatter | solution.py:40
  487.4 9.4 %collective-permute-start = (f32[128,512]{1,0:T(8,128)}, f32[128,512]{1,0:T(8,128)S(1)}, u32[]{:S(2)}, u32[]{:S(2)}) collective-permute-start(f32[128,512]{1,0:T(8,128)} %get-tuple-element.343), channel_id=1, source_target_pairs={{0,24},{8,0},{16,8},{24,16},{1,25},{9,1},{17,9},{25,17},{2,26},{10... | collective-permute-start | bytes 786440 | tf_op jit(solution)/shard_map/while/body/eval_jaxpr/ppermute | solution.py:12
  524.3 65.0 %reduce-scatter.5.cloned.1.call-start = ((), (), s32[]{:S(2)}) async-start(), calls=%async_computation.3 | async-start | bytes 1310720 | tf_op jit(solution)/shard_map/while/body/eval_jaxpr/reduce_scatter | solution.py:58
  549.6 39.7 %copy-start.2 = (f32[1,512]{1,0:T(1,128)S(1)}, f32[1,512]{1,0:T(1,128)}, u32[]{:S(2)}) copy-start(f32[1,512]{1,0:T(1,128)} %get-tuple-element.364) | copy-start | bytes 6148 | tf_op jit(solution)/shard_map/while
  605.9 45.5 %reduce-scatter.3.cloned.1.call-start = ((), (), s32[]{:S(2)}) async-start(), calls=%async_computation.2 | async-start | bytes 2752512 | tf_op jit(solution)/shard_map/while/body/eval_jaxpr/reduce_scatter | solution.py:40
  605.9 9.4 %collective-permute-start = (f32[128,512]{1,0:T(8,128)}, f32[128,512]{1,0:T(8,128)S(1)}, u32[]{:S(2)}, u32[]{:S(2)}) collective-permute-start(f32[128,512]{1,0:T(8,128)} %get-tuple-element.343), channel_id=1, source_target_pairs={{0,24},{8,0},{16,8},{24,16},{1,25},{9,1},{17,9},{25,17},{2,26},{10... | collective-permute-start | bytes 786440 | tf_op jit(solution)/shard_map/while/body/eval_jaxpr/ppermute | solution.py:12
  642.8 65.0 %reduce-scatter.5.cloned.1.call-start = ((), (), s32[]{:S(2)}) async-start(), calls=%async_computation.3 | async-start | bytes 1310720 | tf_op jit(solution)/shard_map/while/body/eval_jaxpr/reduce_scatter | solution.py:58
  668.1 39.7 %copy-start.2 = (f32[1,512]{1,0:T(1,128)S(1)}, f32[1,512]{1,0:T(1,128)}, u32[]{:S(2)}) copy-start(f32[1,512]{1,0:T(1,128)} %get-tuple-element.364) | copy-start | bytes 6148 | tf_op jit(solution)/shard_map/while
  724.4 45.5 %reduce-scatter.3.cloned.1.call-start = ((), (), s32[]{:S(2)}) async-start(), calls=%async_computation.2 | async-start | bytes 2752512 | tf_op jit(solution)/shard_map/while/body/eval_jaxpr/reduce_scatter | solution.py:40
  724.4 9.4 %collective-permute-start = (f32[128,512]{1,0:T(8,128)}, f32[128,512]{1,0:T(8,128)S(1)}, u32[]{:S(2)}, u32[]{:S(2)}) collective-permute-start(f32[128,512]{1,0:T(8,128)} %get-tuple-element.343), channel_id=1, source_target_pairs={{0,24},{8,0},{16,8},{24,16},{1,25},{9,1},{17,9},{25,17},{2,26},{10... | collective-permute-start | bytes 786440 | tf_op jit(solution)/shard_map/while/body/eval_jaxpr/ppermute | solution.py:12
  761.3 65.0 %reduce-scatter.5.cloned.1.call-start = ((), (), s32[]{:S(2)}) async-start(), calls=%async_computation.3 | async-start | bytes 1310720 | tf_op jit(solution)/shard_map/while/body/eval_jaxpr/reduce_scatter | solution.py:58
  786.6 39.7 %copy-start.2 = (f32[1,512]{1,0:T(1,128)S(1)}, f32[1,512]{1,0:T(1,128)}, u32[]{:S(2)}) copy-start(f32[1,512]{1,0:T(1,128)} %get-tuple-element.364) | copy-start | bytes 6148 | tf_op jit(solution)/shard_map/while
  842.9 9.4 %collective-permute-start.1 = (f32[128,512]{1,0:T(8,128)}, f32[128,512]{1,0:T(8,128)S(1)}, u32[]{:S(2)}, u32[]{:S(2)}) collective-permute-start(f32[128,512]{1,0:T(8,128)} %get-tuple-element.223), channel_id=1, source_target_pairs={{0,24},{8,0},{16,8},{24,16},{1,25},{9,1},{17,9},{25,17},{2,26},{10... | collective-permute-start | bytes 786440 | tf_op jit(solution)/shard_map/ppermute | solution.py:12
  853.4 20.6 %copy-start.1 = (f32[128,512]{1,0:T(8,128)}, f32[128,512]{1,0:T(8,128)S(1)}, u32[]{:S(2)}) copy-start(f32[128,512]{1,0:T(8,128)S(1)} %fusion.20) | copy-start | bytes 786436
Sparse Core Ops, SparseCore 0:
  46.7 11.8 reduce-scatter.2
  86.5 28.5 reduce-scatter.4
  168.7 8.5 reduce-scatter.2
  205.1 28.5 reduce-scatter.4
  287.3 8.4 reduce-scatter.2
  323.6 28.5 reduce-scatter.4
  405.9 8.4 reduce-scatter.2
  442.2 28.5 reduce-scatter.4
  524.4 8.4 reduce-scatter.2
  560.7 28.5 reduce-scatter.4
  642.9 8.4 reduce-scatter.2
  679.2 28.5 reduce-scatter.4
  761.5 8.4 reduce-scatter.2
  797.7 28.5 reduce-scatter.4
where the time goes:
time: 882 us; the launch traced here: 881 us
  waiting for transfers between devices  319 us (36%)
  blocking collectives  256 us (29%)
  matrix products  228 us (26%)
  other arithmetic  39.4 us (4%)
  starting transfers between devices  21 us (2%)
  between operations  13.7 us (2%)
    reduce_scatter x7, waiting for transfers between devices, layer_step(): lax.psum_scatter(first + second, 'col', scatter_dimension=0, tiled=True)  201 us
    all_gather x7, blocking collectives, layer_step(): wide = lax.all_gather(gy, 'col', axis=1, tiled=True)  112 us
    psum x7, blocking collectives, layer_step(): inner = lax.psum(jnp.sum(scaled * xf, axis=1), ('row', 'col'))[:, None] / D  95.9 us
    dot_general x7, matrix products, layer_step(): lax.dot_general(wide, wd, (((1,), (1,)), ((), ())), preferred_element_typ...  79.4 us
    dot_general x7, matrix products, layer_step(): lax.dot_general(wu, grad_up, (((1,), (1,)), ((), ())), preferred_element_...  76.5 us
    dot_general x7, matrix products, layer_step(): lax.dot_general(wg, grad_gate, (((1,), (1,)), ((), ())), preferred_elemen...  69.4 us
    reduce_scatter x7, waiting for transfers between devices, layer_step(): ga = lax.psum_scatter(ga_part, 'row', scatter_dimension=1, tiled=True)  63.1 us
    ppermute x8, waiting for transfers between devices, shifted(): lax.ppermute(x, axis, [(i, (i + by) % devices) for i in range(devices)])  54.8 us
  transfers between devices with their start and end apart: 22, of which 22 were waited for; matrix products, arithmetic and copies ran while one was open for 0% of the time, Pallas kernels for 0%

commit v1 on v0

--- a/solution.py
+++ b/solution.py
@@ -33,7 +33,14 @@
         hpair = lax.dynamic_index_in_dim(hidden_all, micro, 0, keepdims=False)
         sumsq = lax.psum(jnp.sum(xf * xf, axis=1), ("row", "col"))
         gy = carry.astype(jnp.bfloat16)
-        wide = lax.all_gather(gy, "col", axis=1, tiled=True)
+        ring = [gy]
+        for hop in range(3):
+            ring.append(lax.ppermute(ring[-1], "col", [(dev, (dev + 1) % 4) for dev in range(4)]))
+        wide = jnp.roll(
+            jnp.concatenate(ring[::-1], axis=1),
+            (lax.axis_index("col") + 1) * ring[0].shape[1],
+            axis=1,
+        )
         ga_part = lax.dot_general(
             wide, wd, (((1,), (1,)), ((), ())), preferred_element_type=jnp.float32
         )

time: 882 us -> 915 us (1.037)
  waiting for transfers between devices: 319 us -> 459 us
  blocking collectives: 256 us -> 144 us
    ppermute x0 -> x21, waiting for transfers between devices: none -> 144 us  [layer_step(): lax.ppermute(ring[-1], 'col', [(dev, (dev + 1) % 4) for dev in range(4)])]
    all_gather x7 -> x0, blocking collectives: 112 us -> none  [layer_step(): wide = lax.all_gather(gy, 'col', axis=1, tiled=True)]
  transfers between devices with their start and end apart: 22 -> 43, of which waited for: 22 -> 43; matrix products, arithmetic and copies ran while one was open for 0% -> 0% of each run, Pallas kernels for 0% -> 0%
where the time goes in v1:
time: 915 us; the launch traced here: 913 us
  waiting for transfers between devices  459 us (50%)
  matrix products  229 us (25%)
  blocking collectives  144 us (16%)
  other arithmetic  40.9 us (4%)
  starting transfers between devices  22.9 us (3%)
  between operations  13.7 us (1%)
    reduce_scatter x7, waiting for transfers between devices, layer_step(): lax.psum_scatter(first + second, 'col', scatter_dimension=0, tiled=True)  201 us
    ppermute x21, waiting for transfers between devices, layer_step(): lax.ppermute(ring[-1], 'col', [(dev, (dev + 1) % 4) for dev in range(4)])  144 us
    psum x7, blocking collectives, layer_step(): inner = lax.psum(jnp.sum(scaled * xf, axis=1), ('row', 'col'))[:, None] / D  95.9 us
    dot_general x7, matrix products, layer_step(): lax.dot_general(wide, wd, (((1,), (1,)), ((), ())), preferred_element_typ...  79.8 us
    dot_general x7, matrix products, layer_step(): lax.dot_general(wu, grad_up, (((1,), (1,)), ((), ())), preferred_element_...  77.1 us
    dot_general x7, matrix products, layer_step(): lax.dot_general(wg, grad_gate, (((1,), (1,)), ((), ())), preferred_elemen...  69.4 us
    reduce_scatter x7, waiting for transfers between devices, layer_step(): ga = lax.psum_scatter(ga_part, 'row', scatter_dimension=1, tiled=True)  58.8 us
    ppermute x8, waiting for transfers between devices, shifted(): lax.ppermute(x, axis, [(i, (i + by) % devices) for i in range(devices)])  54.8 us
  transfers between devices with their start and end apart: 43, of which 43 were waited for; matrix products, arithmetic and copies ran while one was open for 0% of the time, Pallas kernels for 0%

profile of v1, /device:TPU:0, one launch (start us, length us, event | category | flops | bytes accessed | tf_op | source)
XLA Modules:
  0.0 913.0 jit_solution(5801019085201198227)
XLA Ops:
  11.2 864.3 %while.16 = (s32[]{:T(128)}, f32[128,512]{1,0:T(8,128)}, s32[]{:T(128)}, f32[4,128,512]{2,1,0:T(8,128)}, f32[1,512]{1,0:T(1,128)}, /*index=5*/bf16[3584,2048]{1,...) while((s32[]{:T(128)}, f32[128,512]{1,0:T(8,128)}, ...), condition=%wide.region_7.8_spmd, body=%wide.region_0.7_spmd.sunk | while | flops 5641830912 | bytes 80236528 | solution.py:73
  27.8 6.8 collective-permute-done.2
  34.6 6.8 collective-permute-done.3
  41.5 11.4 %fusion.49 = f32[128,3584]{1,0:T(8,128)} fusion(bf16[3584,2048]{1,0:T(8,128)(2,1)} %get-tuple-element.407, bf16[128,4096]{1,0:T(8,128)(2,1)S(1)} %constant_dynamic-update-slice_fusion.23, s32[]{:T(128)S(6)} %select_n.117), kind=kOutput, calls=%fused_computation.15.clone.1 | convolution fusion | flops 1879048192 | bytes 17039364 | tf_op jit(solution)/shard_map/while/body/eval_jaxpr/dot_general | solution.py:44
  53.0 8.4 reduce-scatter.3.cloned.1.call-done
  68.2 9.9 %fusion.51 = f32[128,2048]{1,0:T(8,128)S(1)} fusion(bf16[128,3584]{1,0:T(8,128)(2,1)S(1)} %all_gather.24, bf16[2048,3584]{1,0:T(8,128)(2,1)} %get-tuple-element.409), kind=kOutput, calls=%fused_computation.51.clone.1 | convolution fusion | flops 1879048192 | bytes 16646144 | tf_op jit(solution)/shard_map/while/body/eval_jaxpr/dot_general | solution.py:59
  78.2 11.0 %fusion.52 = f32[2048,128]{0,1:T(8,128)} fusion(f32[128,2048]{1,0:T(8,128)S(1)} %fusion.51, bf16[128,3584]{1,0:T(8,128)(2,1)S(1)} %all_gather.25, bf16[2048,3584]{1,0:T(8,128)(2,1)} %get-tuple-element.410), kind=kOutput, calls=%fused_computation.1.clone.1 | convolution fusion | flops 1879310336 | bytes 17694720 | tf_op jit(solution)/shard_map/while/body/eval_jaxpr/dot_general | solution.py:62
  89.2 28.7 %reduce-scatter.5.cloned.1.call-done = f32[512,128]{0,1:T(8,128)} async-done(((f32[2048,128]{0,1:T(8,128)}), f32[512,128]{0,1:T(8,128)}) %reduce-scatter.5.cloned.1.call-update) | async-done | bytes 262160 | tf_op jit(solution)/shard_map/while/body/eval_jaxpr/reduce_scatter | solution.py:65
  119.0 13.7 %all-reduce.2 = (f32[128]{0:T(128)S(1)}, f32[128]{0:T(128)S(1)}) all-reduce(f32[128]{0:T(128)S(1)} %get-tuple-element.349, f32[128]{0:T(128)S(1)} %get-tuple-element.350), channel_id=1, replica_groups=mesh['section'=4,'row'=2,'col'=4] {'row','col'}, use_global_device_ids=true, to_apply=%region_6.6 | all-reduce | flops 256 | bytes 2048 | tf_op jit(solution)/shard_map/while/body/eval_jaxpr/psum | solution.py:68
  136.9 7.0 collective-permute-done
  144.0 7.4 collective-permute-done.1
  151.4 6.8 collective-permute-done.2
  165.0 11.4 %fusion.49 = f32[128,3584]{1,0:T(8,128)} fusion(bf16[3584,2048]{1,0:T(8,128)(2,1)} %get-tuple-element.407, bf16[128,4096]{1,0:T(8,128)(2,1)S(1)} %constant_dynamic-update-slice_fusion.23, s32[]{:T(128)S(6)} %select_n.117), kind=kOutput, calls=%fused_computation.15.clone.1 | convolution fusion | flops 1879048192 | bytes 17039364 | tf_op jit(solution)/shard_map/while/body/eval_jaxpr/dot_general | solution.py:44
  176.5 8.4 reduce-scatter.3.cloned.1.call-done
  191.7 9.9 %fusion.51 = f32[128,2048]{1,0:T(8,128)S(1)} fusion(bf16[128,3584]{1,0:T(8,128)(2,1)S(1)} %all_gather.24, bf16[2048,3584]{1,0:T(8,128)(2,1)} %get-tuple-element.409), kind=kOutput, calls=%fused_computation.51.clone.1 | convolution fusion | flops 1879048192 | bytes 16646144 | tf_op jit(solution)/shard_map/while/body/eval_jaxpr/dot_general | solution.py:59
  201.7 11.0 %fusion.52 = f32[2048,128]{0,1:T(8,128)} fusion(f32[128,2048]{1,0:T(8,128)S(1)} %fusion.51, bf16[128,3584]{1,0:T(8,128)(2,1)S(1)} %all_gather.25, bf16[2048,3584]{1,0:T(8,128)(2,1)} %get-tuple-element.410), kind=kOutput, calls=%fused_computation.1.clone.1 | convolution fusion | flops 1879310336 | bytes 17694720 | tf_op jit(solution)/shard_map/while/body/eval_jaxpr/dot_general | solution.py:62
  212.7 28.7 %reduce-scatter.5.cloned.1.call-done = f32[512,128]{0,1:T(8,128)} async-done(((f32[2048,128]{0,1:T(8,128)}), f32[512,128]{0,1:T(8,128)}) %reduce-scatter.5.cloned.1.call-update) | async-done | bytes 262160 | tf_op jit(solution)/shard_map/while/body/eval_jaxpr/reduce_scatter | solution.py:65
  242.5 13.7 %all-reduce.2 = (f32[128]{0:T(128)S(1)}, f32[128]{0:T(128)S(1)}) all-reduce(f32[128]{0:T(128)S(1)} %get-tuple-element.349, f32[128]{0:T(128)S(1)} %get-tuple-element.350), channel_id=1, replica_groups=mesh['section'=4,'row'=2,'col'=4] {'row','col'}, use_global_device_ids=true, to_apply=%region_6.6 | all-reduce | flops 256 | bytes 2048 | tf_op jit(solution)/shard_map/while/body/eval_jaxpr/psum | solution.py:68
  260.4 7.0 collective-permute-done
  267.5 7.4 collective-permute-done.1
  288.5 11.4 %fusion.49 = f32[128,3584]{1,0:T(8,128)} fusion(bf16[3584,2048]{1,0:T(8,128)(2,1)} %get-tuple-element.407, bf16[128,4096]{1,0:T(8,128)(2,1)S(1)} %constant_dynamic-update-slice_fusion.23, s32[]{:T(128)S(6)} %select_n.117), kind=kOutput, calls=%fused_computation.15.clone.1 | convolution fusion | flops 1879048192 | bytes 17039364 | tf_op jit(solution)/shard_map/while/body/eval_jaxpr/dot_general | solution.py:44
  300.0 8.4 reduce-scatter.3.cloned.1.call-done
  315.2 9.9 %fusion.51 = f32[128,2048]{1,0:T(8,128)S(1)} fusion(bf16[128,3584]{1,0:T(8,128)(2,1)S(1)} %all_gather.24, bf16[2048,3584]{1,0:T(8,128)(2,1)} %get-tuple-element.409), kind=kOutput, calls=%fused_computation.51.clone.1 | convolution fusion | flops 1879048192 | bytes 16646144 | tf_op jit(solution)/shard_map/while/body/eval_jaxpr/dot_general | solution.py:59
  325.2 11.0 %fusion.52 = f32[2048,128]{0,1:T(8,128)} fusion(f32[128,2048]{1,0:T(8,128)S(1)} %fusion.51, bf16[128,3584]{1,0:T(8,128)(2,1)S(1)} %all_gather.25, bf16[2048,3584]{1,0:T(8,128)(2,1)} %get-tuple-element.410), kind=kOutput, calls=%fused_computation.1.clone.1 | convolution fusion | flops 1879310336 | bytes 17694720 | tf_op jit(solution)/shard_map/while/body/eval_jaxpr/dot_general | solution.py:62
  336.2 28.7 %reduce-scatter.5.cloned.1.call-done = f32[512,128]{0,1:T(8,128)} async-done(((f32[2048,128]{0,1:T(8,128)}), f32[512,128]{0,1:T(8,128)}) %reduce-scatter.5.cloned.1.call-update) | async-done | bytes 262160 | tf_op jit(solution)/shard_map/while/body/eval_jaxpr/reduce_scatter | solution.py:65
  366.0 13.7 %all-reduce.2 = (f32[128]{0:T(128)S(1)}, f32[128]{0:T(128)S(1)}) all-reduce(f32[128]{0:T(128)S(1)} %get-tuple-element.349, f32[128]{0:T(128)S(1)} %get-tuple-element.350), channel_id=1, replica_groups=mesh['section'=4,'row'=2,'col'=4] {'row','col'}, use_global_device_ids=true, to_apply=%region_6.6 | all-reduce | flops 256 | bytes 2048 | tf_op jit(solution)/shard_map/while/body/eval_jaxpr/psum | solution.py:68
  383.9 7.0 collective-permute-done
  391.0 7.4 collective-permute-done.1
  405.1 6.8 collective-permute-done.3
  412.0 11.4 %fusion.49 = f32[128,3584]{1,0:T(8,128)} fusion(bf16[3584,2048]{1,0:T(8,128)(2,1)} %get-tuple-element.407, bf16[128,4096]{1,0:T(8,128)(2,1)S(1)} %constant_dynamic-update-slice_fusion.23, s32[]{:T(128)S(6)} %select_n.117), kind=kOutput, calls=%fused_computation.15.clone.1 | convolution fusion | flops 1879048192 | bytes 17039364 | tf_op jit(solution)/shard_map/while/body/eval_jaxpr/dot_general | solution.py:44
  423.5 8.4 reduce-scatter.3.cloned.1.call-done
  438.7 9.9 %fusion.51 = f32[128,2048]{1,0:T(8,128)S(1)} fusion(bf16[128,3584]{1,0:T(8,128)(2,1)S(1)} %all_gather.24, bf16[2048,3584]{1,0:T(8,128)(2,1)} %get-tuple-element.409), kind=kOutput, calls=%fused_computation.51.clone.1 | convolution fusion | flops 1879048192 | bytes 16646144 | tf_op jit(solution)/shard_map/while/body/eval_jaxpr/dot_general | solution.py:59
  448.7 11.0 %fusion.52 = f32[2048,128]{0,1:T(8,128)} fusion(f32[128,2048]{1,0:T(8,128)S(1)} %fusion.51, bf16[128,3584]{1,0:T(8,128)(2,1)S(1)} %all_gather.25, bf16[2048,3584]{1,0:T(8,128)(2,1)} %get-tuple-element.410), kind=kOutput, calls=%fused_computation.1.clone.1 | convolution fusion | flops 1879310336 | bytes 17694720 | tf_op jit(solution)/shard_map/while/body/eval_jaxpr/dot_general | solution.py:62
  459.7 28.7 %reduce-scatter.5.cloned.1.call-done = f32[512,128]{0,1:T(8,128)} async-done(((f32[2048,128]{0,1:T(8,128)}), f32[512,128]{0,1:T(8,128)}) %reduce-scatter.5.cloned.1.call-update) | async-done | bytes 262160 | tf_op jit(solution)/shard_map/while/body/eval_jaxpr/reduce_scatter | solution.py:65
  489.5 13.7 %all-reduce.2 = (f32[128]{0:T(128)S(1)}, f32[128]{0:T(128)S(1)}) all-reduce(f32[128]{0:T(128)S(1)} %get-tuple-element.349, f32[128]{0:T(128)S(1)} %get-tuple-element.350), channel_id=1, replica_groups=mesh['section'=4,'row'=2,'col'=4] {'row','col'}, use_global_device_ids=true, to_apply=%region_6.6 | all-reduce | flops 256 | bytes 2048 | tf_op jit(solution)/shard_map/while/body/eval_jaxpr/psum | solution.py:68
  507.4 7.0 collective-permute-done
  514.5 7.4 collective-permute-done.1
  521.8 6.8 collective-permute-done.2
  528.6 6.8 collective-permute-done.3
  535.5 11.4 %fusion.49 = f32[128,3584]{1,0:T(8,128)} fusion(bf16[3584,2048]{1,0:T(8,128)(2,1)} %get-tuple-element.407, bf16[128,4096]{1,0:T(8,128)(2,1)S(1)} %constant_dynamic-update-slice_fusion.23, s32[]{:T(128)S(6)} %select_n.117), kind=kOutput, calls=%fused_computation.15.clone.1 | convolution fusion | flops 1879048192 | bytes 17039364 | tf_op jit(solution)/shard_map/while/body/eval_jaxpr/dot_general | solution.py:44
  547.0 8.4 reduce-scatter.3.cloned.1.call-done
  562.2 9.9 %fusion.51 = f32[128,2048]{1,0:T(8,128)S(1)} fusion(bf16[128,3584]{1,0:T(8,128)(2,1)S(1)} %all_gather.24, bf16[2048,3584]{1,0:T(8,128)(2,1)} %get-tuple-element.409), kind=kOutput, calls=%fused_computation.51.clone.1 | convolution fusion | flops 1879048192 | bytes 16646144 | tf_op jit(solution)/shard_map/while/body/eval_jaxpr/dot_general | solution.py:59
  572.1 11.0 %fusion.52 = f32[2048,128]{0,1:T(8,128)} fusion(f32[128,2048]{1,0:T(8,128)S(1)} %fusion.51, bf16[128,3584]{1,0:T(8,128)(2,1)S(1)} %all_gather.25, bf16[2048,3584]{1,0:T(8,128)(2,1)} %get-tuple-element.410), kind=kOutput, calls=%fused_computation.1.clone.1 | convolution fusion | flops 1879310336 | bytes 17694720 | tf_op jit(solution)/shard_map/while/body/eval_jaxpr/dot_general | solution.py:62
  583.2 28.7 %reduce-scatter.5.cloned.1.call-done = f32[512,128]{0,1:T(8,128)} async-done(((f32[2048,128]{0,1:T(8,128)}), f32[512,128]{0,1:T(8,128)}) %reduce-scatter.5.cloned.1.call-update) | async-done | bytes 262160 | tf_op jit(solution)/shard_map/while/body/eval_jaxpr/reduce_scatter | solution.py:65
  613.0 13.7 %all-reduce.2 = (f32[128]{0:T(128)S(1)}, f32[128]{0:T(128)S(1)}) all-reduce(f32[128]{0:T(128)S(1)} %get-tuple-element.349, f32[128]{0:T(128)S(1)} %get-tuple-element.350), channel_id=1, replica_groups=mesh['section'=4,'row'=2,'col'=4] {'row','col'}, use_global_device_ids=true, to_apply=%region_6.6 | all-reduce | flops 256 | bytes 2048 | tf_op jit(solution)/shard_map/while/body/eval_jaxpr/psum | solution.py:68
  630.9 7.0 collective-permute-done
  637.9 7.4 collective-permute-done.1
  645.3 6.8 collective-permute-done.2
  659.0 11.4 %fusion.49 = f32[128,3584]{1,0:T(8,128)} fusion(bf16[3584,2048]{1,0:T(8,128)(2,1)} %get-tuple-element.407, bf16[128,4096]{1,0:T(8,128)(2,1)S(1)} %constant_dynamic-update-slice_fusion.23, s32[]{:T(128)S(6)} %select_n.117), kind=kOutput, calls=%fused_computation.15.clone.1 | convolution fusion | flops 1879048192 | bytes 17039364 | tf_op jit(solution)/shard_map/while/body/eval_jaxpr/dot_general | solution.py:44
  670.5 8.4 reduce-scatter.3.cloned.1.call-done
  685.7 9.9 %fusion.51 = f32[128,2048]{1,0:T(8,128)S(1)} fusion(bf16[128,3584]{1,0:T(8,128)(2,1)S(1)} %all_gather.24, bf16[2048,3584]{1,0:T(8,128)(2,1)} %get-tuple-element.409), kind=kOutput, calls=%fused_computation.51.clone.1 | convolution fusion | flops 1879048192 | bytes 16646144 | tf_op jit(solution)/shard_map/while/body/eval_jaxpr/dot_general | solution.py:59
  695.6 11.0 %fusion.52 = f32[2048,128]{0,1:T(8,128)} fusion(f32[128,2048]{1,0:T(8,128)S(1)} %fusion.51, bf16[128,3584]{1,0:T(8,128)(2,1)S(1)} %all_gather.25, bf16[2048,3584]{1,0:T(8,128)(2,1)} %get-tuple-element.410), kind=kOutput, calls=%fused_computation.1.clone.1 | convolution fusion | flops 1879310336 | bytes 17694720 | tf_op jit(solution)/shard_map/while/body/eval_jaxpr/dot_general | solution.py:62
  706.7 28.7 %reduce-scatter.5.cloned.1.call-done = f32[512,128]{0,1:T(8,128)} async-done(((f32[2048,128]{0,1:T(8,128)}), f32[512,128]{0,1:T(8,128)}) %reduce-scatter.5.cloned.1.call-update) | async-done | bytes 262160 | tf_op jit(solution)/shard_map/while/body/eval_jaxpr/reduce_scatter | solution.py:65
  736.4 13.7 %all-reduce.2 = (f32[128]{0:T(128)S(1)}, f32[128]{0:T(128)S(1)}) all-reduce(f32[128]{0:T(128)S(1)} %get-tuple-element.349, f32[128]{0:T(128)S(1)} %get-tuple-element.350), channel_id=1, replica_groups=mesh['section'=4,'row'=2,'col'=4] {'row','col'}, use_global_device_ids=true, to_apply=%region_6.6 | all-reduce | flops 256 | bytes 2048 | tf_op jit(solution)/shard_map/while/body/eval_jaxpr/psum | solution.py:68
  754.4 7.0 collective-permute-done
  761.4 7.4 collective-permute-done.1
  782.5 11.4 %fusion.49 = f32[128,3584]{1,0:T(8,128)} fusion(bf16[3584,2048]{1,0:T(8,128)(2,1)} %get-tuple-element.407, bf16[128,4096]{1,0:T(8,128)(2,1)S(1)} %constant_dynamic-update-slice_fusion.23, s32[]{:T(128)S(6)} %select_n.117), kind=kOutput, calls=%fused_computation.15.clone.1 | convolution fusion | flops 1879048192 | bytes 17039364 | tf_op jit(solution)/shard_map/while/body/eval_jaxpr/dot_general | solution.py:44
  794.0 8.4 reduce-scatter.3.cloned.1.call-done
  809.2 9.9 %fusion.51 = f32[128,2048]{1,0:T(8,128)S(1)} fusion(bf16[128,3584]{1,0:T(8,128)(2,1)S(1)} %all_gather.24, bf16[2048,3584]{1,0:T(8,128)(2,1)} %get-tuple-element.409), kind=kOutput, calls=%fused_computation.51.clone.1 | convolution fusion | flops 1879048192 | bytes 16646144 | tf_op jit(solution)/shard_map/while/body/eval_jaxpr/dot_general | solution.py:59
  819.1 11.0 %fusion.52 = f32[2048,128]{0,1:T(8,128)} fusion(f32[128,2048]{1,0:T(8,128)S(1)} %fusion.51, bf16[128,3584]{1,0:T(8,128)(2,1)S(1)} %all_gather.25, bf16[2048,3584]{1,0:T(8,128)(2,1)} %get-tuple-element.410), kind=kOutput, calls=%fused_computation.1.clone.1 | convolution fusion | flops 1879310336 | bytes 17694720 | tf_op jit(solution)/shard_map/while/body/eval_jaxpr/dot_general | solution.py:62
  830.2 28.7 %reduce-scatter.5.cloned.1.call-done = f32[512,128]{0,1:T(8,128)} async-done(((f32[2048,128]{0,1:T(8,128)}), f32[512,128]{0,1:T(8,128)}) %reduce-scatter.5.cloned.1.call-update) | async-done | bytes 262160 | tf_op jit(solution)/shard_map/while/body/eval_jaxpr/reduce_scatter | solution.py:65
  859.9 13.7 %all-reduce.2 = (f32[128]{0:T(128)S(1)}, f32[128]{0:T(128)S(1)}) all-reduce(f32[128]{0:T(128)S(1)} %get-tuple-element.349, f32[128]{0:T(128)S(1)} %get-tuple-element.350), channel_id=1, replica_groups=mesh['section'=4,'row'=2,'col'=4] {'row','col'}, use_global_device_ids=true, to_apply=%region_6.6 | all-reduce | flops 256 | bytes 2048 | tf_op jit(solution)/shard_map/while/body/eval_jaxpr/psum | solution.py:68
  877.8 7.0 collective-permute-done.4
  887.9 14.0 %psum.37 = f32[8]{0:T(128)S(1)} all-reduce(f32[8]{0:T(128)S(1)} %fusion.19), channel_id=1, replica_groups=mesh['section'=4,'row'=2,'col'=4] {'row','col'}, use_global_device_ids=true, to_apply=%region_8.9 | all-reduce | flops 8 | bytes 64 | tf_op jit(solution)/shard_map/psum | solution.py:77
  (209 shorter events, 161.9 us)
Async XLA Ops:
  7.2 894.8 %copy-start = (f32[1,8,128,512]{3,2,1,0:T(8,128)S(1)}, f32[1,8,128,512]{3,2,1,0:T(8,128)}, u32[]{:S(2)}) copy-start(f32[1,8,128,512]{3,2,1,0:T(8,128)} %param.14) | copy-start | bytes 6291460
  11.2 50.3 %reduce-scatter.3.cloned.1.call-start = ((), (), s32[]{:S(2)}) async-start(), calls=%async_computation.2 | async-start | bytes 2752512 | tf_op jit(solution)/shard_map/while/body/eval_jaxpr/reduce_scatter | solution.py:47
  11.2 9.8 %collective-permute-start = (f32[128,512]{1,0:T(8,128)}, f32[128,512]{1,0:T(8,128)S(1)}, u32[]{:S(2)}, u32[]{:S(2)}) collective-permute-start(f32[128,512]{1,0:T(8,128)} %get-tuple-element.380), channel_id=1, source_target_pairs={{0,24},{8,0},{16,8},{24,16},{1,25},{9,1},{17,9},{25,17},{2,26},{10... | collective-permute-start | bytes 786440 | tf_op jit(solution)/shard_map/while/body/eval_jaxpr/ppermute | solution.py:12
  21.0 6.8 collective-permute-start.1
  27.8 6.8 collective-permute-start.2
  34.6 6.8 collective-permute-start.3
  52.9 65.0 %reduce-scatter.5.cloned.1.call-start = ((), (), s32[]{:S(2)}) async-start(), calls=%async_computation.3 | async-start | bytes 1310720 | tf_op jit(solution)/shard_map/while/body/eval_jaxpr/reduce_scatter | solution.py:65
  78.2 39.8 %copy-start.1 = (f32[4,128,512]{2,1,0:T(8,128)S(1)}, f32[4,128,512]{2,1,0:T(8,128)}, u32[]{:S(2)}) copy-start(f32[4,128,512]{2,1,0:T(8,128)} %get-tuple-element.405) | copy-start | bytes 3145732 | tf_op jit(solution)/shard_map/while
  78.2 39.8 %copy-start.3 = (f32[1,512]{1,0:T(1,128)S(1)}, f32[1,512]{1,0:T(1,128)}, u32[]{:S(2)}) copy-start(f32[1,512]{1,0:T(1,128)} %get-tuple-element.406) | copy-start | bytes 6148 | tf_op jit(solution)/shard_map/while
  134.5 50.4 %reduce-scatter.3.cloned.1.call-start = ((), (), s32[]{:S(2)}) async-start(), calls=%async_computation.2 | async-start | bytes 2752512 | tf_op jit(solution)/shard_map/while/body/eval_jaxpr/reduce_scatter | solution.py:47
  134.5 9.4 %collective-permute-start = (f32[128,512]{1,0:T(8,128)}, f32[128,512]{1,0:T(8,128)S(1)}, u32[]{:S(2)}, u32[]{:S(2)}) collective-permute-start(f32[128,512]{1,0:T(8,128)} %get-tuple-element.380), channel_id=1, source_target_pairs={{0,24},{8,0},{16,8},{24,16},{1,25},{9,1},{17,9},{25,17},{2,26},{10... | collective-permute-start | bytes 786440 | tf_op jit(solution)/shard_map/while/body/eval_jaxpr/ppermute | solution.py:12
  143.9 7.4 collective-permute-start.1
  151.3 6.8 collective-permute-start.2
  158.1 6.8 collective-permute-start.3
  176.5 65.0 %reduce-scatter.5.cloned.1.call-start = ((), (), s32[]{:S(2)}) async-start(), calls=%async_computation.3 | async-start | bytes 1310720 | tf_op jit(solution)/shard_map/while/body/eval_jaxpr/reduce_scatter | solution.py:65
  201.7 39.8 %copy-start.1 = (f32[4,128,512]{2,1,0:T(8,128)S(1)}, f32[4,128,512]{2,1,0:T(8,128)}, u32[]{:S(2)}) copy-start(f32[4,128,512]{2,1,0:T(8,128)} %get-tuple-element.405) | copy-start | bytes 3145732 | tf_op jit(solution)/shard_map/while
  201.7 39.8 %copy-start.3 = (f32[1,512]{1,0:T(1,128)S(1)}, f32[1,512]{1,0:T(1,128)}, u32[]{:S(2)}) copy-start(f32[1,512]{1,0:T(1,128)} %get-tuple-element.406) | copy-start | bytes 6148 | tf_op jit(solution)/shard_map/while
  258.0 50.4 %reduce-scatter.3.cloned.1.call-start = ((), (), s32[]{:S(2)}) async-start(), calls=%async_computation.2 | async-start | bytes 2752512 | tf_op jit(solution)/shard_map/while/body/eval_jaxpr/reduce_scatter | solution.py:47
  258.0 9.4 %collective-permute-start = (f32[128,512]{1,0:T(8,128)}, f32[128,512]{1,0:T(8,128)S(1)}, u32[]{:S(2)}, u32[]{:S(2)}) collective-permute-start(f32[128,512]{1,0:T(8,128)} %get-tuple-element.380), channel_id=1, source_target_pairs={{0,24},{8,0},{16,8},{24,16},{1,25},{9,1},{17,9},{25,17},{2,26},{10... | collective-permute-start | bytes 786440 | tf_op jit(solution)/shard_map/while/body/eval_jaxpr/ppermute | solution.py:12
  267.4 7.4 collective-permute-start.1
  274.8 6.8 collective-permute-start.2
  281.6 6.8 collective-permute-start.3
  300.0 65.0 %reduce-scatter.5.cloned.1.call-start = ((), (), s32[]{:S(2)}) async-start(), calls=%async_computation.3 | async-start | bytes 1310720 | tf_op jit(solution)/shard_map/while/body/eval_jaxpr/reduce_scatter | solution.py:65
  325.1 39.8 %copy-start.1 = (f32[4,128,512]{2,1,0:T(8,128)S(1)}, f32[4,128,512]{2,1,0:T(8,128)}, u32[]{:S(2)}) copy-start(f32[4,128,512]{2,1,0:T(8,128)} %get-tuple-element.405) | copy-start | bytes 3145732 | tf_op jit(solution)/shard_map/while
  325.2 39.8 %copy-start.3 = (f32[1,512]{1,0:T(1,128)S(1)}, f32[1,512]{1,0:T(1,128)}, u32[]{:S(2)}) copy-start(f32[1,512]{1,0:T(1,128)} %get-tuple-element.406) | copy-start | bytes 6148 | tf_op jit(solution)/shard_map/while
  381.5 50.4 %reduce-scatter.3.cloned.1.call-start = ((), (), s32[]{:S(2)}) async-start(), calls=%async_computation.2 | async-start | bytes 2752512 | tf_op jit(solution)/shard_map/while/body/eval_jaxpr/reduce_scatter | solution.py:47
  381.5 9.4 %collective-permute-start = (f32[128,512]{1,0:T(8,128)}, f32[128,512]{1,0:T(8,128)S(1)}, u32[]{:S(2)}, u32[]{:S(2)}) collective-permute-start(f32[128,512]{1,0:T(8,128)} %get-tuple-element.380), channel_id=1, source_target_pairs={{0,24},{8,0},{16,8},{24,16},{1,25},{9,1},{17,9},{25,17},{2,26},{10... | collective-permute-start | bytes 786440 | tf_op jit(solution)/shard_map/while/body/eval_jaxpr/ppermute | solution.py:12
  390.9 7.4 collective-permute-start.1
  398.3 6.8 collective-permute-start.2
  405.1 6.8 collective-permute-start.3
  423.4 65.0 %reduce-scatter.5.cloned.1.call-start = ((), (), s32[]{:S(2)}) async-start(), calls=%async_computation.3 | async-start | bytes 1310720 | tf_op jit(solution)/shard_map/while/body/eval_jaxpr/reduce_scatter | solution.py:65
  448.6 39.8 %copy-start.1 = (f32[4,128,512]{2,1,0:T(8,128)S(1)}, f32[4,128,512]{2,1,0:T(8,128)}, u32[]{:S(2)}) copy-start(f32[4,128,512]{2,1,0:T(8,128)} %get-tuple-element.405) | copy-start | bytes 3145732 | tf_op jit(solution)/shard_map/while
  448.6 39.8 %copy-start.3 = (f32[1,512]{1,0:T(1,128)S(1)}, f32[1,512]{1,0:T(1,128)}, u32[]{:S(2)}) copy-start(f32[1,512]{1,0:T(1,128)} %get-tuple-element.406) | copy-start | bytes 6148 | tf_op jit(solution)/shard_map/while
  505.0 50.4 %reduce-scatter.3.cloned.1.call-start = ((), (), s32[]{:S(2)}) async-start(), calls=%async_computation.2 | async-start | bytes 2752512 | tf_op jit(solution)/shard_map/while/body/eval_jaxpr/reduce_scatter | solution.py:47
  505.0 9.4 %collective-permute-start = (f32[128,512]{1,0:T(8,128)}, f32[128,512]{1,0:T(8,128)S(1)}, u32[]{:S(2)}, u32[]{:S(2)}) collective-permute-start(f32[128,512]{1,0:T(8,128)} %get-tuple-element.380), channel_id=1, source_target_pairs={{0,24},{8,0},{16,8},{24,16},{1,25},{9,1},{17,9},{25,17},{2,26},{10... | collective-permute-start | bytes 786440 | tf_op jit(solution)/shard_map/while/body/eval_jaxpr/ppermute | solution.py:12
  514.4 7.4 collective-permute-start.1
  521.8 6.8 collective-permute-start.2
  528.6 6.8 collective-permute-start.3
  546.9 65.0 %reduce-scatter.5.cloned.1.call-start = ((), (), s32[]{:S(2)}) async-start(), calls=%async_computation.3 | async-start | bytes 1310720 | tf_op jit(solution)/shard_map/while/body/eval_jaxpr/reduce_scatter | solution.py:65
  572.1 39.8 %copy-start.1 = (f32[4,128,512]{2,1,0:T(8,128)S(1)}, f32[4,128,512]{2,1,0:T(8,128)}, u32[]{:S(2)}) copy-start(f32[4,128,512]{2,1,0:T(8,128)} %get-tuple-element.405) | copy-start | bytes 3145732 | tf_op jit(solution)/shard_map/while
  572.1 39.8 %copy-start.3 = (f32[1,512]{1,0:T(1,128)S(1)}, f32[1,512]{1,0:T(1,128)}, u32[]{:S(2)}) copy-start(f32[1,512]{1,0:T(1,128)} %get-tuple-element.406) | copy-start | bytes 6148 | tf_op jit(solution)/shard_map/while
  628.5 50.4 %reduce-scatter.3.cloned.1.call-start = ((), (), s32[]{:S(2)}) async-start(), calls=%async_computation.2 | async-start | bytes 2752512 | tf_op jit(solution)/shard_map/while/body/eval_jaxpr/reduce_scatter | solution.py:47
  628.5 9.4 %collective-permute-start = (f32[128,512]{1,0:T(8,128)}, f32[128,512]{1,0:T(8,128)S(1)}, u32[]{:S(2)}, u32[]{:S(2)}) collective-permute-start(f32[128,512]{1,0:T(8,128)} %get-tuple-element.380), channel_id=1, source_target_pairs={{0,24},{8,0},{16,8},{24,16},{1,25},{9,1},{17,9},{25,17},{2,26},{10... | collective-permute-start | bytes 786440 | tf_op jit(solution)/shard_map/while/body/eval_jaxpr/ppermute | solution.py:12
  637.9 7.4 collective-permute-start.1
  645.3 6.8 collective-permute-start.2
  652.1 6.8 collective-permute-start.3
  670.4 65.0 %reduce-scatter.5.cloned.1.call-start = ((), (), s32[]{:S(2)}) async-start(), calls=%async_computation.3 | async-start | bytes 1310720 | tf_op jit(solution)/shard_map/while/body/eval_jaxpr/reduce_scatter | solution.py:65
  695.6 39.8 %copy-start.1 = (f32[4,128,512]{2,1,0:T(8,128)S(1)}, f32[4,128,512]{2,1,0:T(8,128)}, u32[]{:S(2)}) copy-start(f32[4,128,512]{2,1,0:T(8,128)} %get-tuple-element.405) | copy-start | bytes 3145732 | tf_op jit(solution)/shard_map/while
  695.6 39.8 %copy-start.3 = (f32[1,512]{1,0:T(1,128)S(1)}, f32[1,512]{1,0:T(1,128)}, u32[]{:S(2)}) copy-start(f32[1,512]{1,0:T(1,128)} %get-tuple-element.406) | copy-start | bytes 6148 | tf_op jit(solution)/shard_map/while
  752.0 50.4 %reduce-scatter.3.cloned.1.call-start = ((), (), s32[]{:S(2)}) async-start(), calls=%async_computation.2 | async-start | bytes 2752512 | tf_op jit(solution)/shard_map/while/body/eval_jaxpr/reduce_scatter | solution.py:47
  752.0 9.4 %collective-permute-start = (f32[128,512]{1,0:T(8,128)}, f32[128,512]{1,0:T(8,128)S(1)}, u32[]{:S(2)}, u32[]{:S(2)}) collective-permute-start(f32[128,512]{1,0:T(8,128)} %get-tuple-element.380), channel_id=1, source_target_pairs={{0,24},{8,0},{16,8},{24,16},{1,25},{9,1},{17,9},{25,17},{2,26},{10... | collective-permute-start | bytes 786440 | tf_op jit(solution)/shard_map/while/body/eval_jaxpr/ppermute | solution.py:12
  761.4 7.4 collective-permute-start.1
  768.8 6.8 collective-permute-start.2
  775.5 6.8 collective-permute-start.3
  793.9 65.0 %reduce-scatter.5.cloned.1.call-start = ((), (), s32[]{:S(2)}) async-start(), calls=%async_computation.3 | async-start | bytes 1310720 | tf_op jit(solution)/shard_map/while/body/eval_jaxpr/reduce_scatter | solution.py:65
  819.1 39.8 %copy-start.1 = (f32[4,128,512]{2,1,0:T(8,128)S(1)}, f32[4,128,512]{2,1,0:T(8,128)}, u32[]{:S(2)}) copy-start(f32[4,128,512]{2,1,0:T(8,128)} %get-tuple-element.405) | copy-start | bytes 3145732 | tf_op jit(solution)/shard_map/while
  819.1 39.8 %copy-start.3 = (f32[1,512]{1,0:T(1,128)S(1)}, f32[1,512]{1,0:T(1,128)}, u32[]{:S(2)}) copy-start(f32[1,512]{1,0:T(1,128)} %get-tuple-element.406) | copy-start | bytes 6148 | tf_op jit(solution)/shard_map/while
  875.5 9.4 %collective-permute-start.4 = (f32[128,512]{1,0:T(8,128)}, f32[128,512]{1,0:T(8,128)S(1)}, u32[]{:S(2)}, u32[]{:S(2)}) collective-permute-start(f32[128,512]{1,0:T(8,128)} %get-tuple-element.255), channel_id=1, source_target_pairs={{0,24},{8,0},{16,8},{24,16},{1,25},{9,1},{17,9},{25,17},{2,26},{10... | collective-permute-start | bytes 786440 | tf_op jit(solution)/shard_map/ppermute | solution.py:12
  885.9 20.6 %copy-start.2 = (f32[128,512]{1,0:T(8,128)}, f32[128,512]{1,0:T(8,128)S(1)}, u32[]{:S(2)}) copy-start(f32[128,512]{1,0:T(8,128)S(1)} %fusion.23) | copy-start | bytes 786436
Sparse Core Ops, SparseCore 0:
  53.1 8.3 reduce-scatter.2
  89.3 28.5 reduce-scatter.4
  176.6 8.3 reduce-scatter.2
  212.8 28.5 reduce-scatter.4
  300.1 8.3 reduce-scatter.2
  336.3 28.5 reduce-scatter.4
  423.6 8.3 reduce-scatter.2
  459.8 28.5 reduce-scatter.4
  547.0 8.3 reduce-scatter.2
  583.3 28.5 reduce-scatter.4
  670.5 8.3 reduce-scatter.2
  706.8 28.5 reduce-scatter.4
  794.0 8.3 reduce-scatter.2
  830.3 28.5 reduce-scatter.4
